TPU v7x, 128 devices: a whole 4x4x4 slice. The times are simulated.
128 devices in a mesh: cls: 8 (over y, core), mem: 16 (over z, x).
Axes of the slice: x: 4, y: 4, z: 4, core: 2. Of those that a mesh axis runs over, the one named last changes fastest.
Arguments:
- images: bfloat16 [3072, 65536], P(('cls', 'mem')), may hold values from -6 to 6
- owner_group: int32 [3072, 1], P(('cls', 'mem')), may hold values from 0 to 7; in each aligned block of 24 rows (0 to 23, 24 to 47, ...) at most 6 rows name the same one
- bin_in_group: int32 [3072], P(('cls', 'mem')), may hold values from 0 to 7
- defocus: bfloat16 [3072], P(('cls', 'mem')), may hold values from 0.5 to 2
- projections: bfloat16 [64, 65536], P('cls'), may hold values from -6 to 6
- sketch_weight: bfloat16 [64, 48], replicated, may hold values from -0.875 to 0.875
Outputs:
- basis: bfloat16 [8, 64, 65536], P('cls', None, 'mem')
Inputs may be any that keep to these rules, and one draw needn't show every extreme that they name: `owner_group`: in the particles of one device no class group is named more than 6 times, and 6 is reached on some device.
All inputs are finite; a program needn't handle non-finite values.
Results may differ from a plain program's by a relative error of at most 0.012.
The roundings to bfloat16 on the way count: a program that leaves them out, or rounds other values in their place, can miss the bound.
Values may be sent and summed in bfloat16 or wider, within the bound.
A program may use at most 128 MiB of HBM per device.

v0:
```python
import jax
import jax.numpy as jnp
from jax import lax
from jax.sharding import PartitionSpec as P

SIDE = 256
CAP = 6


def swapped(value, axis, bit):
    return lax.ppermute(value, axis, [(i, i ^ 1 << bit) for i in range(lax.axis_size(axis))])


def wave_grid(side):
    position = jnp.arange(side * side, dtype=jnp.int32)
    column = position % side
    row_idx = position // side
    fx = jnp.where(column < side // 2, column, column - side).astype(jnp.float32) / side
    fy = jnp.where(row_idx < side // 2, row_idx, row_idx - side).astype(jnp.float32) / side
    return 160.0 * (fx * fx + fy * fy)


def coefficients(gram, pixels):
    total = jnp.trace(gram) + 1e-06
    scaled = gram / total
    ident = jnp.eye(gram.shape[0], dtype=jnp.float32)
    first = 1.5 * ident - 0.5 * scaled
    later = jnp.dot(
        jnp.dot(first, scaled, precision=lax.Precision.HIGHEST),
        first,
        precision=lax.Precision.HIGHEST,
    )
    second = 1.5 * ident - 0.5 * later
    coef = jnp.dot(second, first, precision=lax.Precision.HIGHEST) * jnp.sqrt(pixels / total)
    return coef.astype(jnp.bfloat16)


def self_gram(matrix):
    return jnp.einsum("kp,jp->kj", matrix, matrix, preferred_element_type=jnp.float32)


def norm_basis(matrix):
    coef = coefficients(self_gram(matrix), float(matrix.shape[1]))
    return jnp.dot(coef, matrix, preferred_element_type=jnp.float32).astype(jnp.bfloat16)


def body(images, owner_group, bin_in_group, defocus, projections, sketch_weight):
    n_cls = lax.axis_size("cls")
    n_mem = lax.axis_size("mem")
    levels = n_mem.bit_length() - 1
    pixels = images.shape[1]
    width = pixels // n_mem
    member = lax.axis_index("mem")
    bins_here = projections.shape[0]
    owners = owner_group[:, 0]
    onehot = (owners[:, None] == jnp.arange(n_cls, dtype=jnp.int32)[None, :]).astype(jnp.int32)
    before = jnp.cumsum(onehot, axis=0) - onehot
    rank = jnp.sum(onehot * before, axis=1)
    target = owners * CAP + rank
    select = jnp.arange(n_cls * CAP, dtype=jnp.int32)[:, None] == target[None, :]
    sent_images = jnp.dot(
        select.astype(jnp.bfloat16), images, preferred_element_type=jnp.float32
    ).astype(jnp.bfloat16)
    meta_source = jnp.stack(
        [defocus.astype(jnp.float32), (bin_in_group + 1).astype(jnp.float32)], axis=1
    )
    meta = jnp.dot(select.astype(jnp.float32), meta_source, precision=lax.Precision.HIGHEST)
    meta = jnp.stack([meta[:, 0], meta[:, 1] - 1.0], axis=1).astype(jnp.bfloat16)
    got_images, got_meta = (
        lax.all_to_all(sent_images, "cls", split_axis=0, concat_axis=0, tiled=True),
        lax.all_to_all(meta, "cls", split_axis=0, concat_axis=0, tiled=True),
    )
    focus = got_meta[:, 0].astype(jnp.float32)
    local_bin = got_meta[:, 1].astype(jnp.float32)
    bin_table = (local_bin[:, None] == jnp.arange(bins_here, dtype=jnp.float32)[None, :]).astype(
        jnp.bfloat16
    )
    chosen = jnp.dot(bin_table, projections, preferred_element_type=jnp.float32)
    chi = focus[:, None] * wave_grid(SIDE)[None, :]
    ctf = -(jnp.sin(chi) + 0.1 * jnp.cos(chi))
    residual = (got_images.astype(jnp.float32) - ctf * chosen).astype(jnp.bfloat16)
    sketch = jnp.dot(sketch_weight, residual, preferred_element_type=jnp.float32).astype(
        jnp.bfloat16
    )
    current = norm_basis(sketch)
    for level in range(levels):
        partner = swapped(current, "mem", level)
        joined = (current.astype(jnp.float32) + partner.astype(jnp.float32)).astype(jnp.bfloat16)
        current = norm_basis(joined)
    result = lax.dynamic_slice_in_dim(current, member * width, width, 1)
    return result[None]


def solution(mesh):
    in_specs = (
        P(("cls", "mem"), None),
        P(("cls", "mem"), None),
        P(("cls", "mem")),
        P(("cls", "mem")),
        P("cls", None),
        P(),
    )
    out_specs = P("cls", None, "mem")
    return jax.shard_map(body, mesh=mesh, in_specs=in_specs, out_specs=out_specs, check_vma=False)
```

profile of v0, /device:TPU:0, one launch (start us, length us, event | category | flops | bytes accessed | tf_op | source)
XLA Modules:
  0.0 1044.5 jit_solution(18058357614809266810)
XLA Ops:
  4.7 4.6 all-to-all-start.1
  9.3 4.5 convolution_convert_fusion.5
  13.8 6.3 all_to_all.12
  20.1 5.0 all-to-all-start
  25.4 94.3 %all-to-all-done = bf16[8,6,65536]{2,1,0:T(8,128)(2,1)} async-done(((bf16[8,6,65536]{2,1,0:T(8,128)(2,1)}), bf16[8,6,65536]{2,1,0:T(8,128)(2,1)}, u32[]{:S(2)}, u32[]{:S(2)}) %all-to-all-start) | async-done | bytes 6291488 | tf_op jit(solution)/shard_map/all_to_all | solution.py:70
  119.7 11.6 %reshape.52 = f32[48,65536]{1,0:T(8,128)} reshape(bf16[8,6,65536]{2,1,0:T(8,128)(2,1)} %all-to-all-done) | data formatting | bytes 18874368 | tf_op jit(solution)/shard_map/convert_element_type | solution.py:81
  131.3 53.3 %convolution_convert_fusion.4 = bf16[65536,64]{0,1:T(8,128)(2,1)} fusion(bf16[64,48]{0,1:T(8,128)(2,1)S(1)} %copy-done.4, f32[48,65536]{1,0:T(8,128)} %reshape.52, bf16[8,65536]{1,0:T(8,128)(2,1)S(1)} %copy-done.3, f32[65536]{0:T(1024)S(1)} %fusion.32, f32[48]{0:T(128)S(1)} %get-tuple-element.6, f32[48]{0:T(128)S(1)} %get-tuple-element.5), kind=kOutput, calls=%fused_computation.4 | convolution fusion | flops 479199616 | bytes 22288768 | tf_op jit(solution)/shard_map/dot_general | solution.py:82
  184.6 8.8 select_reduce_fusion.4
  194.7 5.7 convolution_convert_fusion.3
  200.4 3.2 copy-done.2
  205.1 180.6 %collective-permute-done = bf16[64,65536]{1,0:T(8,128)(2,1)} collective-permute-done((bf16[64,65536]{1,0:T(8,128)(2,1)S(1)}, bf16[64,65536]{1,0:T(8,128)(2,1)}, u32[]{:S(2)}, u32[]{:S(2)}) %collective-permute-start) | collective-permute-done | bytes 8388640 | tf_op jit(solution)/shard_map/ppermute | solution.py:11
  385.7 15.0 %select_reduce_fusion.3 = (f32[]{:T(128)}, f32[64,64]{1,0:T(8,128)S(1)}) fusion(bf16[64,65536]{1,0:T(8,128)(2,1)} %collective-permute-done, bf16[64,65536]{1,0:T(8,128)(2,1)} %copy-done.2), kind=kOutput, calls=%fused_computation.78 | convolution fusion | flops 553660416 | bytes 16793604 | tf_op jit(solution)/shard_map/kp,jp->kj/dot_general | solution.py:39
  402.0 11.3 %convolution_convert_fusion.2 = bf16[64,65536]{1,0:T(8,128)(2,1)} fusion(bf16[64,64]{1,0:T(8,128)(2,1)S(1)} %fusion.16, bf16[64,65536]{1,0:T(8,128)(2,1)} %collective-permute-done, bf16[64,65536]{1,0:T(8,128)(2,1)} %copy-done.2), kind=kOutput, calls=%fused_computation.2 | convolution fusion | flops 557842432 | bytes 25174016 | tf_op jit(solution)/shard_map/dot_general | solution.py:44
  413.4 3.4 collective-permute-start.1
  416.8 179.9 %collective-permute-done.1 = bf16[64,65536]{1,0:T(8,128)(2,1)} collective-permute-done((bf16[64,65536]{1,0:T(8,128)(2,1)}, bf16[64,65536]{1,0:T(8,128)(2,1)}, u32[]{:S(2)}, u32[]{:S(2)}) %collective-permute-start.1) | collective-permute-done | bytes 8388640 | tf_op jit(solution)/shard_map/ppermute | solution.py:11
  596.7 15.0 %select_reduce_fusion.2 = (f32[]{:T(128)}, f32[64,64]{1,0:T(8,128)S(1)}) fusion(bf16[64,65536]{1,0:T(8,128)(2,1)} %collective-permute-done.1, bf16[64,65536]{1,0:T(8,128)(2,1)} %convolution_convert_fusion.2), kind=kOutput, calls=%fused_computation.76 | convolution fusion | flops 553660416 | bytes 16793604 | tf_op jit(solution)/shard_map/kp,jp->kj/dot_general | solution.py:39
  613.0 11.3 %convolution_convert_fusion.1 = bf16[64,65536]{1,0:T(8,128)(2,1)} fusion(bf16[64,64]{1,0:T(8,128)(2,1)S(1)} %fusion.17, bf16[64,65536]{1,0:T(8,128)(2,1)} %collective-permute-done.1, bf16[64,65536]{1,0:T(8,128)(2,1)} %convolution_convert_fusion.2), kind=kOutput, calls=%fused_computation.1 | convolution fusion | flops 557842432 | bytes 25174016 | tf_op jit(solution)/shard_map/dot_general | solution.py:44
  626.4 178.7 %collective-permute-done.2 = bf16[64,65536]{1,0:T(8,128)(2,1)} collective-permute-done((bf16[64,65536]{1,0:T(8,128)(2,1)}, bf16[64,65536]{1,0:T(8,128)(2,1)}, u32[]{:S(2)}, u32[]{:S(2)}) %collective-permute-start.2) | collective-permute-done | bytes 8388640 | tf_op jit(solution)/shard_map/ppermute | solution.py:11
  805.2 15.0 %select_reduce_fusion.1 = (f32[]{:T(128)}, f32[64,64]{1,0:T(8,128)S(1)}) fusion(bf16[64,65536]{1,0:T(8,128)(2,1)} %collective-permute-done.2, bf16[64,65536]{1,0:T(8,128)(2,1)} %convolution_convert_fusion.1), kind=kOutput, calls=%fused_computation.74 | convolution fusion | flops 553660416 | bytes 16793604 | tf_op jit(solution)/shard_map/kp,jp->kj/dot_general | solution.py:39
  821.5 11.3 %convolution_convert_fusion = bf16[64,65536]{1,0:T(8,128)(2,1)} fusion(bf16[64,64]{1,0:T(8,128)(2,1)S(1)} %fusion.18, bf16[64,65536]{1,0:T(8,128)(2,1)} %collective-permute-done.2, bf16[64,65536]{1,0:T(8,128)(2,1)} %convolution_convert_fusion.1), kind=kOutput, calls=%fused_computation | convolution fusion | flops 557842432 | bytes 25174016 | tf_op jit(solution)/shard_map/dot_general | solution.py:44
  832.8 3.9 collective-permute-start.3
  836.7 177.8 %collective-permute-done.3 = bf16[64,65536]{1,0:T(8,128)(2,1)} collective-permute-done((bf16[64,65536]{1,0:T(8,128)(2,1)}, bf16[64,65536]{1,0:T(8,128)(2,1)}, u32[]{:S(2)}, u32[]{:S(2)}) %collective-permute-start.3) | collective-permute-done | bytes 8388640 | tf_op jit(solution)/shard_map/ppermute | solution.py:11
  1014.5 15.0 %select_reduce_fusion = (f32[]{:T(128)}, f32[64,64]{1,0:T(8,128)S(1)}) fusion(bf16[64,65536]{1,0:T(8,128)(2,1)} %collective-permute-done.3, bf16[64,65536]{1,0:T(8,128)(2,1)} %convolution_convert_fusion), kind=kOutput, calls=%fused_computation.72 | convolution fusion | flops 553660416 | bytes 16793604 | tf_op jit(solution)/shard_map/kp,jp->kj/dot_general | solution.py:39
  1030.9 11.5 %fusion.8 = bf16[64,65536]{1,0:T(8,128)(2,1)} fusion(bf16[64,64]{1,0:T(8,128)(2,1)S(1)} %fusion.19, bf16[64,65536]{1,0:T(8,128)(2,1)} %collective-permute-done.3, bf16[64,65536]{1,0:T(8,128)(2,1)} %convolution_convert_fusion), kind=kOutput, calls=%fused_computation.21 | convolution fusion | flops 553648128 | bytes 25174016 | tf_op jit(solution)/shard_map/dot_general | solution.py:44
  (44 shorter events, 13.0 us)
Async XLA Ops:
  0.0 9.3 copy-start
  4.7 15.3 %all-to-all-start.1 = ((bf16[8,6,2]{1,2,0:T(2,128)(2,1)}), bf16[8,6,2]{1,2,0:T(2,128)(2,1)S(1)}, u32[]{:S(2)}, u32[]{:S(2)}) async-start(bf16[8,6,2]{1,2,0:T(2,128)(2,1)} %copy.7), calls=%async_computation.1 | async-start | bytes 8192 | tf_op jit(solution)/shard_map/all_to_all | solution.py:71
  20.1 99.6 %all-to-all-start = ((bf16[8,6,65536]{2,1,0:T(8,128)(2,1)}), bf16[8,6,65536]{2,1,0:T(8,128)(2,1)}, u32[]{:S(2)}, u32[]{:S(2)}) async-start(bf16[8,6,65536]{2,1,0:T(8,128)(2,1)} %all_to_all.12), calls=%async_computation | async-start | bytes 16777216 | tf_op jit(solution)/shard_map/all_to_all | solution.py:70
  25.3 106.0 %copy-start.3 = (bf16[8,65536]{1,0:T(8,128)(2,1)S(1)}, bf16[8,65536]{1,0:T(8,128)(2,1)}, u32[]{:S(2)}) copy-start(bf16[8,65536]{1,0:T(8,128)(2,1)} %param.10) | copy-start | bytes 3145732
  25.3 105.9 %copy-start.4 = (bf16[64,48]{0,1:T(8,128)(2,1)S(1)}, bf16[64,48]{0,1:T(8,128)(2,1)}, u32[]{:S(2)}) copy-start(bf16[64,48]{0,1:T(8,128)(2,1)} %param.11) | copy-start | bytes 18436
  200.4 3.2 copy-start.2
  203.6 182.1 %collective-permute-start = (bf16[64,65536]{1,0:T(8,128)(2,1)S(1)}, bf16[64,65536]{1,0:T(8,128)(2,1)}, u32[]{:S(2)}, u32[]{:S(2)}) collective-permute-start(bf16[64,65536]{1,0:T(8,128)(2,1)S(1)} %convolution_convert_fusion.3), channel_id=1, source_target_pairs={{0,1},{1,0},{2,3},{3,2},{4,5},{5,4},{6,7},{7,6},{8,9},{9,8},{10,11... | collective-permute-start | bytes 25165832 | tf_op jit(solution)/shard_map/ppermute | solution.py:11
  413.4 183.3 %collective-permute-start.1 = (bf16[64,65536]{1,0:T(8,128)(2,1)}, bf16[64,65536]{1,0:T(8,128)(2,1)}, u32[]{:S(2)}, u32[]{:S(2)}) collective-permute-start(bf16[64,65536]{1,0:T(8,128)(2,1)} %convolution_convert_fusion.2), channel_id=1, source_target_pairs={{0,2},{1,3},{2,0},{3,1},{4,6},{5,7},{6,4},{7,5},{8,10},{9,11},{10,... | collective-permute-start | bytes 25165832 | tf_op jit(solution)/shard_map/ppermute | solution.py:11
  624.3 180.8 %collective-permute-start.2 = (bf16[64,65536]{1,0:T(8,128)(2,1)}, bf16[64,65536]{1,0:T(8,128)(2,1)}, u32[]{:S(2)}, u32[]{:S(2)}) collective-permute-start(bf16[64,65536]{1,0:T(8,128)(2,1)} %convolution_convert_fusion.1), channel_id=1, source_target_pairs={{0,4},{1,5},{2,6},{3,7},{4,0},{5,1},{6,2},{7,3},{8,12},{9,13},{10,... | collective-permute-start | bytes 25165832 | tf_op jit(solution)/shard_map/ppermute | solution.py:11
  832.8 181.7 %collective-permute-start.3 = (bf16[64,65536]{1,0:T(8,128)(2,1)}, bf16[64,65536]{1,0:T(8,128)(2,1)}, u32[]{:S(2)}, u32[]{:S(2)}) collective-permute-start(bf16[64,65536]{1,0:T(8,128)(2,1)} %convolution_convert_fusion), channel_id=1, source_target_pairs={{0,8},{1,9},{2,10},{3,11},{4,12},{5,13},{6,14},{7,15},{8,0},{9,1},... | collective-permute-start | bytes 25165832 | tf_op jit(solution)/shard_map/ppermute | solution.py:11
  1030.7 13.6 %copy-start.1 = (bf16[24,65536]{1,0:T(8,128)(2,1)S(1)}, bf16[24,65536]{1,0:T(8,128)(2,1)}, u32[]{:S(2)}) copy-start(bf16[24,65536]{1,0:T(8,128)(2,1)} %param.6) | copy-start | bytes 9437188
where the time goes:
time: 1050 us; the launch traced here: 1040 us
  waiting for transfers between devices  811 us (77%)
  matrix products  181 us (17%)
  local copies, waits for them, and re-layouts  23.8 us (2%)
  starting transfers between devices  20.5 us (2%)
    ppermute x4, waiting for transfers between devices, swapped(): lax.ppermute(value, axis, [(i, i ^ 1 << bit) for i in range(lax.axis_size...  717 us
    all_to_all x1, waiting for transfers between devices, body(): lax.all_to_all(sent_images, 'cls', split_axis=0, concat_axis=0, tiled=True)  94.3 us
    dot_general x5, matrix products, self_gram(): jnp.einsum('kp,jp->kj', matrix, matrix, preferred_element_type=jnp.float32)  69 us
    dot_general x1, matrix products, body(): jnp.dot(sketch_weight, residual, preferred_element_type=jnp.float32)  53.3 us
    dot_general x5, matrix products, norm_basis(): jnp.dot(coef, matrix, preferred_element_type=jnp.float32)  51.2 us
  transfers between devices with their start and end apart: 6, of which 5 were waited for; matrix products, arithmetic and copies ran while one was open for 0% of the time, Pallas kernels for 0%

commit v1 on v0

v1 whole, which is shorter than its diff:
```python
import math

import jax
import jax.numpy as jnp
from jax import lax
from jax.sharding import PartitionSpec as P

SIDE = 256
CAP = 6
HI = lax.Precision.HIGHEST


def wave_slice(first, width):
    position = first + jnp.arange(width, dtype=jnp.int32)
    column = position % SIDE
    row_idx = position // SIDE
    fx = jnp.where(column < SIDE // 2, column, column - SIDE).astype(jnp.float32) / SIDE
    fy = jnp.where(row_idx < SIDE // 2, row_idx, row_idx - SIDE).astype(jnp.float32) / SIDE
    return 160.0 * (fx * fx + fy * fy)


def bmm(a, b):
    return jnp.einsum("nij,njk->nik", a, b, precision=HI)


def coefficients(gram, pixels):
    total = jnp.trace(gram, axis1=1, axis2=2)[:, None, None] + 1e-06
    scaled = gram / total
    ident = jnp.eye(gram.shape[1], dtype=jnp.float32)[None]
    first = 1.5 * ident - 0.5 * scaled
    later = bmm(bmm(first, scaled), first)
    second = 1.5 * ident - 0.5 * later
    return bmm(second, first) * jnp.sqrt(pixels / total)


def tree(gram, n_mem, rank, pixels):
    blocks = n_mem
    k = gram.reshape(n_mem, rank, n_mem, rank)
    chain = None
    while True:
        diag = jnp.stack([k[i, :, i, :] for i in range(blocks)])
        c = coefficients(diag, pixels)
        if chain is None:
            chain = c[:, :, None, :]
        else:
            chain = jnp.einsum("nij,njmk->nimk", c, chain, precision=HI)
        if blocks == 1:
            return chain.reshape(rank, n_mem * rank)
        k = jnp.einsum("aij,ajbk->aibk", c, k, precision=HI)
        k = jnp.einsum("aibk,blk->aibl", k, c, precision=HI)
        half = blocks // 2
        k = k.reshape(half, 2, rank, half, 2, rank).sum(axis=(1, 4))
        chain = chain.reshape(half, 2, rank, -1, rank).transpose(0, 2, 1, 3, 4).reshape(half, rank, -1, rank)
        blocks = half


def body(images, owner_group, bin_in_group, defocus, projections, sketch_weight):
    n_cls = lax.axis_size("cls")
    n_mem = lax.axis_size("mem")
    pixels = images.shape[1]
    width = pixels // n_mem
    member = lax.axis_index("mem")
    cls = lax.axis_index("cls")
    p_dev = images.shape[0]
    bins_here = projections.shape[0]
    rank_k = sketch_weight.shape[0]
    owners = owner_group[:, 0]
    onehot = (owners[:, None] == jnp.arange(n_cls, dtype=jnp.int32)[None, :]).astype(jnp.int32)
    before = jnp.cumsum(onehot, axis=0) - onehot
    rank = jnp.sum(onehot * before, axis=1)
    target = owners * CAP + rank
    meta = jnp.stack([target.astype(jnp.float32), defocus.astype(jnp.float32), bin_in_group.astype(jnp.float32)])
    meta = lax.all_gather(meta, ("cls", "mem"), tiled=False).reshape(n_cls, n_mem, 3, p_dev)
    rows = lax.all_to_all(images, "mem", split_axis=1, concat_axis=0, tiled=True)
    rows = rows.reshape(n_mem, p_dev, width)
    mine = lax.dynamic_index_in_dim(meta, cls, 0, keepdims=False)[:, 0]
    select = jnp.arange(n_cls * CAP, dtype=jnp.float32)[None, :, None] == mine[:, None, :]
    sent = jnp.einsum("mti,mip->mtp", select.astype(jnp.bfloat16), rows, preferred_element_type=jnp.float32).astype(jnp.bfloat16)
    sent = sent.reshape(n_mem, n_cls, CAP, width).transpose(1, 0, 2, 3).reshape(n_cls * n_mem * CAP, width)
    got = lax.all_to_all(sent, "cls", split_axis=0, concat_axis=0, tiled=True)
    slot = (cls * CAP + jnp.arange(CAP, dtype=jnp.int32)).astype(jnp.float32)
    pick = (slot[None, None, :, None] == meta[:, :, None, 0, :]).astype(jnp.float32)
    focus = jnp.sum(pick * meta[:, :, None, 1, :], axis=-1).reshape(-1)
    local_bin = jnp.sum(pick * meta[:, :, None, 2, :], axis=-1)
    valid = jnp.sum(pick, axis=-1)
    bins = jnp.arange(bins_here, dtype=jnp.float32)
    table = jnp.where((local_bin[..., None] == bins) & (valid[..., None] > 0.5), 1.0, 0.0)
    table = table.reshape(-1, bins_here).astype(jnp.bfloat16)
    proj = lax.dynamic_slice_in_dim(projections, member * width, width, 1)
    chosen = jnp.dot(table, proj, preferred_element_type=jnp.float32)
    chi = focus[:, None] * wave_slice(member * width, width)[None, :]
    ctf = -math.sqrt(1.01) * jnp.sin(chi + math.atan(0.1))
    residual = (got.astype(jnp.float32) - ctf * chosen).astype(jnp.bfloat16)
    residual = residual.reshape(n_cls, n_mem, CAP, width).transpose(1, 0, 2, 3).reshape(n_mem, n_cls * CAP, width)
    sketch = jnp.einsum("ks,msp->mkp", sketch_weight, residual, preferred_element_type=jnp.float32).astype(jnp.bfloat16)
    sketch = sketch.reshape(n_mem * rank_k, width)
    gram = jnp.einsum("ap,bp->ab", sketch, sketch, preferred_element_type=jnp.float32)
    gram = lax.psum(gram, "mem")
    coef = tree(gram, n_mem, rank_k, float(pixels)).astype(jnp.bfloat16)
    result = jnp.dot(coef, sketch, preferred_element_type=jnp.float32).astype(jnp.bfloat16)
    return result[None]


def solution(mesh):
    in_specs = (
        P(("cls", "mem"), None),
        P(("cls", "mem"), None),
        P(("cls", "mem")),
        P(("cls", "mem")),
        P("cls", None),
        P(),
    )
    out_specs = P("cls", None, "mem")
    return jax.shard_map(body, mesh=mesh, in_specs=in_specs, out_specs=out_specs, check_vma=False)
```

time: 1050 us -> 557 us (0.53)
  waiting for transfers between devices: 811 us -> 210 us
  blocking collectives: 0 us -> 96.6 us
  matrix products: 181 us -> 135 us
  local copies, waits for them, and re-layouts: 23.8 us -> 69.5 us
  between operations: 4.14 us -> 15.1 us
    ppermute x4 -> x0, waiting for transfers between devices: 717 us -> none  [swapped(): lax.ppermute(value, axis, [(i, i ^ 1 << bit) for i in range(lax.axis_size...]
    psum x0 -> x1, waiting for transfers between devices: none -> 139 us  [body(): gram = lax.psum(gram, 'mem')]
    all_gather x0 -> x1, blocking collectives: none -> 96.6 us  [body(): lax.all_gather(meta, ('cls', 'mem'), tiled=False)]
    dot_general x28 -> x32, matrix products: 181 us -> 135 us  [the longest x1 47.5 us: body(): chosen = jnp.dot(table, proj, preferred_element_type=jnp.float32)]
    reshape x0 -> x3, local copies, waits for them, and re-layouts: none -> 26.6 us  [the longest x2 16.5 us: tree(): k = gram.reshape(n_mem, rank, n_mem, rank)]
    all_to_all x2, waiting for transfers between devices: 94.3 us -> 70.6 us  [the longest x1 70.6 us: body(): got = lax.all_to_all(sent, 'cls', split_axis=0, concat_axis=0, tiled=True)]
    unnamed x10 -> x52, local copies, waits for them, and re-layouts: 3.23 us -> 16.4 us
    ppermute x4 -> x0, starting transfers between devices: 10.9 us -> none  [swapped(): lax.ppermute(value, axis, [(i, i ^ 1 << bit) for i in range(lax.axis_size...]
  transfers between devices with their start and end apart: 6 -> 3, of which waited for: 5 -> 2; matrix products, arithmetic and copies ran while one was open for 0% -> 0% of each run, Pallas kernels for 0% -> 0%
where the time goes in v1:
time: 557 us; the launch traced here: 546 us
  waiting for transfers between devices  210 us (38%)
  matrix products  135 us (24%)
  blocking collectives  96.6 us (17%)
  local copies, waits for them, and re-layouts  69.5 us (12%)
  between operations  15.1 us (3%)
  starting transfers between devices  12.8 us (2%)
  other arithmetic  7.06 us (1%)
    psum x1, waiting for transfers between devices, body(): gram = lax.psum(gram, 'mem')  139 us
    all_gather x1, blocking collectives, body(): lax.all_gather(meta, ('cls', 'mem'), tiled=False)  96.6 us
    all_to_all x1, waiting for transfers between devices, body(): got = lax.all_to_all(sent, 'cls', split_axis=0, concat_axis=0, tiled=True)  70.6 us
    dot_general x1, matrix products, body(): chosen = jnp.dot(table, proj, preferred_element_type=jnp.float32)  47.5 us
    dot_general x4, matrix products, tree(): k = jnp.einsum('aibk,blk->aibl', k, c, precision=HI)  34.3 us
    dot_general x4, matrix products, tree(): k = jnp.einsum('aij,ajbk->aibk', c, k, precision=HI)  16.8 us
    reshape x2, local copies, waits for them, and re-layouts, tree(): k = gram.reshape(n_mem, rank, n_mem, rank)  16.5 us
    unnamed x52, local copies, waits for them, and re-layouts  16.4 us
  transfers between devices with their start and end apart: 3, of which 2 were waited for; matrix products, arithmetic and copies ran while one was open for 0% of the time, Pallas kernels for 0%

profile of v1, /device:TPU:0, one launch (start us, length us, event | category | flops | bytes accessed | tf_op | source)
XLA Modules:
  0.0 546.0 jit_solution(17044176956349966713)
XLA Ops:
  6.5 4.0 copy.191
  10.6 8.0 %all-to-all-start = ((bf16[24,16,4096]{2,0,1:T(8,128)(2,1)}), bf16[24,16,4096]{2,0,1:T(8,128)(2,1)}, u32[]{:S(2)}, u32[]{:S(2)}) async-start(bf16[24,16,4096]{2,0,1:T(8,128)(2,1)} %bitcast.266), calls=%async_computation | async-start | bytes 6291456 | tf_op jit(solution)/shard_map/all_to_all | solution.py:74
  19.0 96.6 %all-gather.1 = f32[128,3,24]{2,1,0:T(4,128)S(1)} all-gather(f32[1,3,24]{2,1,0:T(4,128)S(1)} %maximum_bitcast_fusion), channel_id=2, replica_groups=mesh['cls'=8,'mem'=16] {'cls','mem'}, dimensions={0}, use_global_device_ids=true | all-gather | bytes 37152 | tf_op jit(solution)/shard_map/all_gather | solution.py:73
  115.6 3.8 convolution_convert_fusion.1
  119.4 3.4 copy.115
  122.8 3.4 copy.116
  126.3 6.3 %copy.117 = bf16[8,96,4096]{2,1,0:T(8,128)(2,1)} copy(bf16[8,96,4096]{2,0,1:T(8,128)(2,1)S(1)} %bitcast.264) | data formatting | bytes 12582912 | tf_op jit(solution)/shard_map/all_to_all | solution.py:80
  132.6 4.7 all-to-all-start.1
  138.9 70.6 %all-to-all-done.1 = bf16[8,96,4096]{2,1,0:T(8,128)(2,1)} async-done(((bf16[8,96,4096]{2,1,0:T(8,128)(2,1)}), bf16[8,96,4096]{2,1,0:T(8,128)(2,1)}, u32[]{:S(2)}, u32[]{:S(2)}) %all-to-all-start.1) | async-done | bytes 6291488 | tf_op jit(solution)/shard_map/all_to_all | solution.py:80
  209.5 47.5 %fusion = bf16[768,4096]{1,0:T(8,128)(2,1)} fusion(bf16[768,4096]{1,0:T(8,128)(2,1)} %bitcast.88, f32[4096]{0:T(1024)S(1)} %fusion.85, f32[768]{0:T(1024)S(1)} %mul.219, f32[768]{0:T(1024)S(1)} %eq.134, pred[768]{0:T(1024)(128)(4,1)S(1)} %gt.16, bf16[8,65536]{1,0:T(8,128)(2,1)S(1)} %copy-done, s32[]{:T(128)S(6)} %select_n.80), kind=kOutput, calls=%fused_computation.1 | convolution fusion | flops 72376320 | bytes 12674052 | tf_op jit(solution)/shard_map/dot_general | solution.py:90
  257.0 10.1 %reshape.271 = bf16[8,16,6,4096]{3,2,1,0:T(8,128)(2,1)} reshape(bf16[768,4096]{1,0:T(8,128)(2,1)} %fusion) | data formatting | bytes 12582912 | tf_op jit(solution)/shard_map/reshape | solution.py:94
  267.1 7.0 %copy.125 = bf16[16,8,6,4096]{3,0,2,1:T(8,128)(2,1)S(1)} copy(bf16[16,8,6,4096]{3,2,0,1:T(8,128)(2,1)} %bitcast.261) | data formatting | bytes 12582912 | tf_op jit(solution)/shard_map/transpose | solution.py:94
  274.1 5.7 %convolution_convert_fusion = bf16[16,4096,64]{1,2,0:T(8,128)(2,1)S(1)} fusion(bf16[16,48,4096]{2,0,1:T(8,128)(2,1)S(1)} %bitcast.265, bf16[64,48]{0,1:T(8,128)(2,1)S(1)} %copy-done.4), kind=kOutput, calls=%fused_computation.4 | convolution fusion | flops 406847488 | bytes 14686208 | tf_op jit(solution)/shard_map/ks,msp->mkp/dot_general | solution.py:95
  279.8 3.2 copy-done.2
  283.0 10.8 %fusion.140 = f32[1024,1024]{1,0:T(8,128)} fusion(bf16[1024,4096]{1,0:T(8,128)(2,1)S(1)} %bitcast.259), kind=kOutput, calls=%fused_computation.242 | convolution fusion | flops 8589934592 | bytes 12582912 | tf_op jit(solution)/shard_map/ap,bp->ab/dot_general | solution.py:97
  293.8 7.3 %reshape.274 = f32[16,64,16,64]{3,2,1,0:T(8,128)} reshape(f32[1024,1024]{1,0:T(8,128)} %fusion.140) | data formatting | bytes 8388608 | tf_op jit(solution)/shard_map/reshape | solution.py:38
  301.1 9.2 %copy.127 = f32[16,64,16,64]{3,1,2,0:T(8,128)} copy(f32[16,64,16,64]{3,2,1,0:T(8,128)} %reshape.274) | data formatting | bytes 8388608 | tf_op jit(solution)/shard_map/reshape | solution.py:38
  310.3 139.5 %all-reduce.2.cloned.1.call-done = f32[16,64,16,64]{3,1,2,0:T(8,128)} async-done(((f32[16,64,16,64]{3,1,2,0:T(8,128)}), f32[16,64,16,64]{3,1,2,0:T(8,128)}) %all-reduce.2.cloned.1.call-update) | async-done | bytes 4194320 | tf_op jit(solution)/shard_map/psum | solution.py:98
  465.1 8.7 %fusion.1 = f32[16,64,16,64]{3,1,0,2:T(8,128)S(1)} fusion(f32[16,64,16,64]{3,1,2,0:T(8,128)S(1)} %copy-done.3, f32[16,64,64]{2,1,0:T(8,128)S(1)} %convolution_multiply_fusion), kind=kOutput, calls=%fused_computation.2 | convolution fusion | flops 805306368 | bytes 8650752 | tf_op jit(solution)/shard_map/aij,ajbk->aibk/dot_general | solution.py:49
  473.8 26.4 %fusion.16 = f32[16,64,16,64]{3,1,2,0:T(8,128)} fusion(f32[16,64,16,64]{3,1,0,2:T(8,128)S(1)} %fusion.1, f32[16,64,64]{2,1,0:T(8,128)S(1)} %convolution_multiply_fusion), kind=kOutput, calls=%fused_computation.36 | convolution fusion | flops 805306368 | bytes 8650752 | tf_op jit(solution)/shard_map/aibk,blk->aibl/dot_general | solution.py:50
  500.1 4.6 reduce_sum.131
  507.1 6.1 %fusion.28 = f32[8,64,8,64]{3,1,0,2:T(8,128)S(1)} fusion(f32[8,64,8,64]{1,3,0,2:T(8,128)S(1)} %reduce_sum.131, f32[8,64,64]{2,1,0:T(8,128)S(1)} %convolution_multiply_fusion.2), kind=kOutput, calls=%fused_computation.53 | convolution fusion | flops 201326592 | bytes 2228224 | tf_op jit(solution)/shard_map/aij,ajbk->aibk/dot_general | solution.py:49
  514.6 6.0 %fusion.26 = f32[8,64,8,64]{3,1,2,0:T(8,128)S(1)} fusion(f32[8,64,8,64]{3,1,0,2:T(8,128)S(1)} %fusion.28, f32[8,64,64]{2,1,0:T(8,128)S(1)} %convolution_multiply_fusion.2), kind=kOutput, calls=%fused_computation.51 | convolution fusion | flops 201326592 | bytes 2228224 | tf_op jit(solution)/shard_map/aibk,blk->aibl/dot_general | solution.py:50
  533.0 5.7 %fusion.4 = bf16[1,64,4096]{2,1,0:T(8,128)(2,1)} fusion(bf16[64,1024]{1,0:T(8,128)(2,1)S(1)} %convolution_convert_fusion.3, bf16[1024,4096]{1,0:T(8,128)(2,1)} %bitcast.260), kind=kOutput, calls=%fused_computation.8 | convolution fusion | flops 537133056 | bytes 9043968 | tf_op jit(solution)/shard_map/dot_general | solution.py:100
  (119 shorter events, 32.3 us)
Async XLA Ops:
  6.5 202.9 %copy-start = (bf16[8,65536]{1,0:T(8,128)(2,1)S(1)}, bf16[8,65536]{1,0:T(8,128)(2,1)}, u32[]{:S(2)}) copy-start(bf16[8,65536]{1,0:T(8,128)(2,1)} %param.10) | copy-start | bytes 3145732
  6.5 12.1 %copy-start.5 = (s32[24,1]{0,1:T(1,128)S(1)}, s32[24,1]{0,1:T(1,128)}, u32[]{:S(2)}) copy-start(s32[24,1]{0,1:T(1,128)} %param.7) | copy-start | bytes 292
  6.5 12.4 %copy-start.6 = (s32[24]{0:T(128)S(1)}, s32[24]{0:T(128)}, u32[]{:S(2)}) copy-start(s32[24]{0:T(128)} %param.8) | copy-start | bytes 292
  6.5 12.4 %copy-start.7 = (bf16[24]{0:T(256)(128)(2,1)S(1)}, bf16[24]{0:T(256)(128)(2,1)}, u32[]{:S(2)}) copy-start(bf16[24]{0:T(256)(128)(2,1)} %param.9) | copy-start | bytes 148
  10.6 105.0 %all-to-all-start = ((bf16[24,16,4096]{2,0,1:T(8,128)(2,1)}), bf16[24,16,4096]{2,0,1:T(8,128)(2,1)}, u32[]{:S(2)}, u32[]{:S(2)}) async-start(bf16[24,16,4096]{2,0,1:T(8,128)(2,1)} %bitcast.266), calls=%async_computation | async-start | bytes 6291456 | tf_op jit(solution)/shard_map/all_to_all | solution.py:74
  132.6 76.9 %all-to-all-start.1 = ((bf16[8,96,4096]{2,1,0:T(8,128)(2,1)}), bf16[8,96,4096]{2,1,0:T(8,128)(2,1)}, u32[]{:S(2)}, u32[]{:S(2)}) async-start(bf16[8,96,4096]{2,1,0:T(8,128)(2,1)} %copy.117), calls=%async_computation.1 | async-start | bytes 12582912 | tf_op jit(solution)/shard_map/all_to_all | solution.py:80
  137.3 312.5 %all-reduce.2.cloned.1.call-start = ((), (), s32[]{:S(2)}) async-start(), calls=%async_computation.2 | async-start | bytes 16777216 | tf_op jit(solution)/shard_map/psum | solution.py:98
  267.1 7.0 %copy-start.4 = (bf16[64,48]{0,1:T(8,128)(2,1)S(1)}, bf16[64,48]{0,1:T(8,128)(2,1)}, u32[]{:S(2)}) copy-start(bf16[64,48]{0,1:T(8,128)(2,1)} %param.11) | copy-start | bytes 18436
  279.8 3.2 copy-start.2
  449.8 15.3 %copy-start.3 = (f32[16,64,16,64]{3,1,2,0:T(8,128)S(1)}, f32[16,64,16,64]{3,1,2,0:T(8,128)}, u32[]{:S(2)}) copy-start(f32[16,64,16,64]{3,1,2,0:T(8,128)} %all-reduce.2.cloned.1.call-done) | copy-start | bytes 12582916
  530.2 8.6 %copy-start.1 = (bf16[8,65536]{1,0:T(8,128)(2,1)S(1)}, bf16[8,65536]{1,0:T(8,128)(2,1)}, u32[]{:S(2)}) copy-start(bf16[8,65536]{1,0:T(8,128)(2,1)} %param.10) | copy-start | bytes 3145732
Sparse Core Ops, SparseCore 0:
  310.4 139.3 all-reduce.1
